TPU v7x, 256 devices: a whole 4x4x8 slice. The times are simulated.
256 devices in a mesh: row: 32 (over z, x), feat: 8 (over y, core).
Axes of the slice: x: 4, y: 4, z: 8, core: 2. Of those that a mesh axis runs over, the one named last changes fastest.
Arguments:
- bin_codes: int32 [256, 262144], P(None, 'row'), may hold values from 0 to 31
- gradients: bfloat16 [262144], P('row'), may hold values from -6 to 6
- hessians: bfloat16 [262144], P('row'), may hold values from 0.019897461 to 0.25
- pair_list: int32 [64, 2], replicated, may hold values from 0 to 255, as said below
- owners: int32 [64], replicated, may hold values from 0 to 7, as said below
Outputs:
- cut_table: float32 [128, 1024], P('feat', 'row')
- best_gain: float32 [64], replicated
Inputs may be any that keep to these rules, and one draw needn't show every extreme that they name: `pair_list`: each row holds two different features, the first smaller. `owners`: one index owns exactly 16 pairs in every draw, the others at most that many.
All inputs are finite; a program needn't handle non-finite values.
Results may differ from a plain program's by a relative error of at most 0.0003.
Values sent between devices are 32-bit elements; how exact they have to be, the bound alone decides.
A program may use at most 64 MiB of HBM per device.

v0:
```python
import jax
import jax.numpy as jnp
from jax import lax
from jax.experimental import pallas as pl
from jax.experimental.pallas import tpu as pltpu
from jax.sharding import PartitionSpec as P

BINS = 32
LAMBDA_REG = 1.0
Z = 8
X = 4
FEAT = 8
PAIRS = 8
CHUNKS = 4
STEP = 2048
MESH = pl.DeviceIdType.MESH
Z_STEPS = (4, 3, 5, 2, 6, 1, 7)
PLANE_STEPS = sorted(
    [(dx, df) for dx in range(X) for df in range(FEAT) if (dx, df) != (0, 0)],
    key=lambda s: -(min(s[0], X - s[0]) + min(s[1], FEAT - s[1]) / 2),
)


def kernel(pairs_hbm, owners_hbm, grad_hbm, hess_hbm, codes_hbm, table_ref, best_ref,
           chunks, pairs_ref, owners_ref, grad_ref, hess_ref,
           acc, send, recv, parts, gain_ref, message, inbox,
           code_sem, small_sem, x_send, x_recv, z_send, z_recv, plane_send, plane_recv):
    row = lax.axis_index("row")
    feat = lax.axis_index("feat")
    z = row // X
    x = lax.rem(row, X)
    chunk_width = chunks[0].shape[1]
    width = STEP
    sub = width // 128

    def fetch(c):
        lanes = pl.ds(c * chunk_width, chunk_width)
        return pltpu.make_async_copy(codes_hbm.at[:, lanes], chunks[c], code_sem.at[c])

    small = [pltpu.make_async_copy(src, dst, small_sem.at[i]) for i, (src, dst) in enumerate(
        ((pairs_hbm, pairs_ref), (grad_hbm, grad_ref), (hess_hbm, hess_ref), (owners_hbm, owners_ref)))]
    fetch(0).start()
    for copy in small:
        copy.start()
    for c in range(1, CHUNKS):
        fetch(c).start()

    def z_peer(step):
        return (lax.rem(z + step, Z) * X + x, feat)

    def plane_peer(dx, df):
        return (z * X + lax.rem(x + dx, X), lax.rem(feat + df, FEAT))

    barrier = pltpu.get_barrier_semaphore()
    for step in Z_STEPS:
        pl.semaphore_signal(barrier, inc=1, device_id=z_peer(step), device_id_type=MESH)
    for dx, df in PLANE_STEPS:
        pl.semaphore_signal(barrier, inc=1, device_id=plane_peer(dx, df), device_id_type=MESH)

    level = lax.broadcasted_iota(jnp.int32, (16, width), 0).astype(jnp.float32).astype(jnp.bfloat16)
    level_up = level + jnp.bfloat16(16)
    one = jnp.ones((16, width), jnp.bfloat16)
    zero = jnp.zeros((16, width), jnp.bfloat16)

    def accumulate(c, codes, inner):
        start = inner * width
        block = c * (chunk_width // width) + inner

        def spread(ref):
            rows = ref[pl.ds(block * sub, sub), :].astype(jnp.float32)
            flat = jnp.concatenate([rows[j:j + 1, :] for j in range(sub)], axis=1)
            return jnp.broadcast_to(flat, (16, width)).astype(jnp.bfloat16)

        grad = spread(grad_ref)
        hess = spread(hess_ref)
        streamed, held = [], []
        for i in range(PAIRS):
            p = feat * PAIRS + i
            ca = codes[pl.ds(pairs_ref[0, p], 1), pl.ds(start, width)].astype(jnp.float32)
            cb = codes[pl.ds(pairs_ref[1, p], 1), pl.ds(start, width)].astype(jnp.float32)
            ca = jnp.broadcast_to(ca, (16, width)).astype(jnp.bfloat16)
            cb = jnp.broadcast_to(cb, (16, width)).astype(jnp.bfloat16)
            held += [jnp.where(cb <= level, one, zero), jnp.where(cb <= level_up, one, zero)]
            low, high = ca <= level, ca <= level_up
            streamed += [jnp.where(low, grad, zero), jnp.where(high, grad, zero),
                         jnp.where(low, hess, zero), jnp.where(high, hess, zero)]
        product = lax.dot_general(jnp.concatenate(streamed, axis=0), jnp.concatenate(held, axis=0),
                                  (((1,), (1,)), ((), ())), preferred_element_type=jnp.float32)
        for i in range(PAIRS):
            tile = product[64 * i:64 * i + 64, 128 * (i // 4):128 * (i // 4) + 128]
            acc[i] = tile if block == 0 else acc[i] + tile

    for copy in small:
        copy.wait()
    for c in range(CHUNKS):
        fetch(c).wait()
        for inner in range(chunk_width // width):
            accumulate(c, chunks[c], inner)

    lane = lax.broadcasted_iota(jnp.int32, (BINS, 128), 1)
    for i in range(X):
        both_pairs = [jnp.where(lax.rem(lane, 64) < 32, acc[2 * i, k:k + 32], acc[2 * i + 1, k:k + 32])
                      for k in (0, 32)]
        away = 1 - i % 2
        both_pairs[away] = pltpu.roll(both_pairs[away], 64, 1)
        send[i] = jnp.where(lane < 64, both_pairs[0], both_pairs[1])

    pl.semaphore_wait(barrier, Z - 1 + X * FEAT - 1)

    for dx in (2, 1, 3):
        other = lax.rem(x + dx, X)
        pltpu.make_async_remote_copy(
            src_ref=send.at[other], dst_ref=recv.at[x], send_sem=x_send, recv_sem=x_recv,
            device_id=(z * X + other, feat), device_id_type=MESH).start()

    mine = owners_ref[...] == feat
    mine_value = jnp.where(mine, 1.0, 0.0).astype(jnp.bfloat16)
    before = lax.broadcasted_iota(jnp.int32, (64, 64), 0) < lax.broadcasted_iota(jnp.int32, (64, 64), 1)
    rank = jnp.dot(mine_value, jnp.where(before, 1.0, 0.0).astype(jnp.bfloat16),
                   preferred_element_type=jnp.float32)
    slot = lax.broadcasted_iota(jnp.int32, (16, 64), 0).astype(jnp.float32)
    chosen = jnp.where((jnp.broadcast_to(rank, (16, 64)) == slot) & jnp.broadcast_to(mine, (16, 64)),
                       1.0, 0.0).astype(jnp.bfloat16)
    pair = lax.broadcasted_iota(jnp.int32, (64, 64), 0)
    place = lax.broadcasted_iota(jnp.int32, (64, 64), 1)
    order = jnp.where(pair == 2 * lax.rem(place, 32) + place // 32, 1.0, 0.0).astype(jnp.bfloat16)
    chosen = jnp.dot(chosen, order, preferred_element_type=jnp.float32)

    recv[x] = send[x]
    others = recv.at[pl.ds(0, X - 1)]
    pltpu.make_async_copy(others, others, x_recv).wait()
    parts[z] = jnp.sum(recv[...], axis=0)

    for step in Z_STEPS:
        pltpu.make_async_remote_copy(
            src_ref=parts.at[z], dst_ref=parts.at[z], send_sem=z_send, recv_sem=z_recv,
            device_id=z_peer(step), device_id_type=MESH).start()
    others = parts.at[pl.ds(0, Z - 1)]
    pltpu.make_async_copy(others, others, z_recv).wait()
    total = jnp.sum(parts[...], axis=0)

    def ends(values):
        return jnp.where(lane < 32, jnp.broadcast_to(values[:, 31:32], (BINS, 128)),
                         jnp.broadcast_to(values[:, 63:64], (BINS, 128)))

    grad_cum = total
    hess_cum = pltpu.roll(total, 64, 1)
    grad_end = ends(grad_cum)
    hess_end = ends(hess_cum)
    grad_col = grad_cum[31:32]
    hess_col = hess_cum[31:32]
    grad_all = grad_end[31:32]
    hess_all = hess_end[31:32]
    quad_grad = (grad_cum, grad_end - grad_cum, grad_col - grad_cum, grad_all - grad_end - grad_col + grad_cum)
    quad_hess = (hess_cum, hess_end - hess_cum, hess_col - hess_cum, hess_all - hess_end - hess_col + hess_cum)
    valid = lane < 64
    gain = -(grad_all * grad_all) / (hess_all + LAMBDA_REG)
    for grad_part, hess_part in zip(quad_grad, quad_hess):
        safe = jnp.where(valid, hess_part, 0.0)
        gain = gain + grad_part * grad_part / (safe + LAMBDA_REG)
    gain_ref[...] = gain.reshape(Z, X, 128)
    top = jnp.max(gain, axis=0, keepdims=True)
    lane_row = lane[0:1]
    lowest = jnp.float32(-jnp.inf)
    top_left = jnp.max(jnp.where(lane_row < 32, top, lowest), axis=1, keepdims=True)
    top_right = jnp.max(jnp.where((lane_row >= 32) & (lane_row < 64), top, lowest), axis=1, keepdims=True)
    pair_lane = 64 + feat * PAIRS + 2 * x
    peaks = jnp.where(lane_row == pair_lane, top_left, jnp.where(lane_row == pair_lane + 1, top_right, 0.0))
    own = jnp.where(lane[0:X] < 64, gain_ref[z], peaks)
    message[...] = own.reshape(X, 1, 128)

    here = feat * X + x
    for dx, df in PLANE_STEPS:
        pltpu.make_async_remote_copy(
            src_ref=message.at[lax.rem(x + dx, X)], dst_ref=inbox.at[here],
            send_sem=plane_send, recv_sem=plane_recv,
            device_id=plane_peer(dx, df), device_id_type=MESH).start()
    inbox[here] = message[x]
    others = inbox.at[pl.ds(0, X * FEAT - 1)]
    pltpu.make_async_copy(others, others, plane_recv).wait()
    news = inbox[...].reshape(X * FEAT, 128)
    table_ref[...] = jnp.dot(chosen, jnp.concatenate([news[:, 0:32], news[:, 32:64]], axis=0),
                             precision=lax.Precision.HIGHEST, preferred_element_type=jnp.float32)
    best = jnp.sum(news, axis=0, keepdims=True)
    best_ref[...] = best[:, 64:128]

    sent = recv.at[pl.ds(0, X - 1)]
    pltpu.make_async_copy(sent, sent, x_send).wait()
    sent = parts.at[pl.ds(0, Z - 1)]
    pltpu.make_async_copy(sent, sent, z_send).wait()
    sent = inbox.at[pl.ds(0, X * FEAT - 1)]
    pltpu.make_async_copy(sent, sent, plane_send).wait()


def shards(bin_codes, gradients, hessians, pair_list, owners):
    rows = bin_codes.shape[1]
    anywhere = pl.BlockSpec(memory_space=pl.ANY)
    vmem = pl.BlockSpec(memory_space=pltpu.VMEM)
    table, best = pl.pallas_call(
        kernel,
        out_shape=(pltpu.VMEM((16, BINS), jnp.float32), pltpu.VMEM((1, FEAT * PAIRS), jnp.float32)),
        in_specs=[anywhere] * 5,
        out_specs=(vmem, vmem),
        scratch_shapes=[[pltpu.VMEM((bin_codes.shape[0], rows // CHUNKS), jnp.int32)] * CHUNKS,
            pltpu.SMEM((2, FEAT * PAIRS), jnp.int32),
            pltpu.VMEM((1, FEAT * PAIRS), jnp.int32),
            pltpu.VMEM((rows // 128, 128), jnp.bfloat16),
            pltpu.VMEM((rows // 128, 128), jnp.bfloat16),
            pltpu.VMEM((PAIRS, 64, 128), jnp.float32),
            pltpu.VMEM((X, BINS, 128), jnp.float32),
            pltpu.VMEM((X, BINS, 128), jnp.float32),
            pltpu.VMEM((Z, BINS, 128), jnp.float32),
            pltpu.VMEM((Z, X, 128), jnp.float32),
            pltpu.VMEM((X, 1, 128), jnp.float32),
            pltpu.VMEM((X * FEAT, 1, 128), jnp.float32),
            pltpu.SemaphoreType.DMA((CHUNKS,)),
            pltpu.SemaphoreType.DMA((4,)),
        ] + [pltpu.SemaphoreType.DMA] * 6,
        compiler_params=pltpu.CompilerParams(collective_id=0, has_side_effects=True),
    )(pair_list.T, owners.reshape(1, -1), gradients.reshape(rows // 128, 128),
      hessians.reshape(rows // 128, 128), bin_codes)
    return table, best.reshape(-1)


def solution(mesh):
    in_specs = (P(None, "row"), P("row"), P("row"), P(), P())
    out_specs = (P("feat", "row"), P())
    return jax.shard_map(shards, mesh=mesh, in_specs=in_specs, out_specs=out_specs, check_vma=False)
```

profile of v0, /device:TPU:1, one launch (start us, length us, event | category | flops | bytes accessed | tf_op | source)
XLA Modules:
  0.0 29.9 jit_solution(6010057664843634353)
XLA Ops:
  0.6 28.1 %shard_map.68 = (f32[16,32]{1,0:T(8,128)S(1)}, f32[1,64]{1,0:T(1,128)S(1)}) custom-call(s32[2,64]{1,0:T(2,128)} %bitcast.8, s32[1,64]{1,0:T(1,128)} %bitcast.9, bf16[64,128]{1,0:T(8,128)(2,1)} %bitcast.6, bf16[64,128]{1,0:T(8,128)(2,1)} %bitcast.7, s32[256,8192]{1,0:T(8,128)} %codes_hbm.1), custom_call_target="tpu_custom_call" | custom-call | tf_op jit(solution)/shard_map/pallas_call | solution.py:199
  28.8 0.6 %copy.9 = f32[16,32]{1,0:T(8,128)} copy(f32[16,32]{1,0:T(8,128)S(1)} %get-tuple-element.6) | data formatting | bytes 4096
  29.4 0.5 %copy.10 = f32[64]{0:T(128)} copy(f32[64]{0:T(128)S(1)} %bitcast.5) | data formatting | bytes 512
where the time goes:
time: 30 us; the launch traced here: 29.9 us
  Pallas kernels  28.1 us (94%)
  local copies, waits for them, and re-layouts  1.11 us (4%)
  between operations  0.64 us (2%)
    pallas_call x1, Pallas kernels, shards(): pl.pallas_call(kernel, out_shape=(pltpu.VMEM((16, BINS), jnp.float32), pl...  28.1 us
    unnamed x2, local copies, waits for them, and re-layouts  1.11 us

commit v1 on v0

--- a/solution.py
+++ b/solution.py
@@ -11,8 +11,8 @@
 X = 4
 FEAT = 8
 PAIRS = 8
-CHUNKS = 4
-STEP = 2048
+CHUNKS = (1024, 3072, 4096)
+STEP = 1024
 MESH = pl.DeviceIdType.MESH
 Z_STEPS = (4, 3, 5, 2, 6, 1, 7)
 PLANE_STEPS = sorted(
@@ -29,12 +29,11 @@
     feat = lax.axis_index("feat")
     z = row // X
     x = lax.rem(row, X)
-    chunk_width = chunks[0].shape[1]
     width = STEP
     sub = width // 128
 
     def fetch(c):
-        lanes = pl.ds(c * chunk_width, chunk_width)
+        lanes = pl.ds(sum(CHUNKS[:c]), CHUNKS[c])
         return pltpu.make_async_copy(codes_hbm.at[:, lanes], chunks[c], code_sem.at[c])
 
     small = [pltpu.make_async_copy(src, dst, small_sem.at[i]) for i, (src, dst) in enumerate(
@@ -42,7 +41,7 @@
     fetch(0).start()
     for copy in small:
         copy.start()
-    for c in range(1, CHUNKS):
+    for c in range(1, len(CHUNKS)):
         fetch(c).start()
 
     def z_peer(step):
@@ -64,7 +63,7 @@
 
     def accumulate(c, codes, inner):
         start = inner * width
-        block = c * (chunk_width // width) + inner
+        block = sum(CHUNKS[:c]) // width + inner
 
         def spread(ref):
             rows = ref[pl.ds(block * sub, sub), :].astype(jnp.float32)
@@ -73,37 +72,35 @@
 
         grad = spread(grad_ref)
         hess = spread(hess_ref)
-        streamed, held = [], []
-        for i in range(PAIRS):
-            p = feat * PAIRS + i
-            ca = codes[pl.ds(pairs_ref[0, p], 1), pl.ds(start, width)].astype(jnp.float32)
-            cb = codes[pl.ds(pairs_ref[1, p], 1), pl.ds(start, width)].astype(jnp.float32)
-            ca = jnp.broadcast_to(ca, (16, width)).astype(jnp.bfloat16)
-            cb = jnp.broadcast_to(cb, (16, width)).astype(jnp.bfloat16)
-            held += [jnp.where(cb <= level, one, zero), jnp.where(cb <= level_up, one, zero)]
-            low, high = ca <= level, ca <= level_up
-            streamed += [jnp.where(low, grad, zero), jnp.where(high, grad, zero),
-                         jnp.where(low, hess, zero), jnp.where(high, hess, zero)]
-        product = lax.dot_general(jnp.concatenate(streamed, axis=0), jnp.concatenate(held, axis=0),
-                                  (((1,), (1,)), ((), ())), preferred_element_type=jnp.float32)
-        for i in range(PAIRS):
-            tile = product[64 * i:64 * i + 64, 128 * (i // 4):128 * (i // 4) + 128]
-            acc[i] = tile if block == 0 else acc[i] + tile
+        for group in range(2):
+            first, second = [], []
+            for i in range(4):
+                p = feat * PAIRS + group * 4 + i
+                ca = codes[pl.ds(pairs_ref[0, p], 1), pl.ds(start, width)].astype(jnp.float32)
+                cb = codes[pl.ds(pairs_ref[1, p], 1), pl.ds(start, width)].astype(jnp.float32)
+                ca = jnp.broadcast_to(ca, (16, width)).astype(jnp.bfloat16)
+                cb = jnp.broadcast_to(cb, (16, width)).astype(jnp.bfloat16)
+                first += [jnp.where(ca <= level, one, zero), jnp.where(ca <= level_up, one, zero)]
+                low, high = cb <= level, cb <= level_up
+                second.append([[jnp.where(low, w, zero), jnp.where(high, w, zero)] for w in (grad, hess)])
+            columns = [tile for i in (0, 2) for w in range(2) for j in (i, i + 1) for tile in second[j][w]]
+            product = lax.dot_general(jnp.concatenate(first, axis=0), jnp.concatenate(columns, axis=0),
+                                      (((1,), (1,)), ((), ())), preferred_element_type=jnp.float32)
+            for half in range(2):
+                tile = product[64 * half:64 * half + 64, 128 * half:128 * half + 128]
+                k = 2 * group + half
+                acc[k] = tile if block == 0 else acc[k] + tile
 
     for copy in small:
         copy.wait()
-    for c in range(CHUNKS):
+    for c in range(len(CHUNKS)):
         fetch(c).wait()
-        for inner in range(chunk_width // width):
+        for inner in range(CHUNKS[c] // width):
             accumulate(c, chunks[c], inner)
 
     lane = lax.broadcasted_iota(jnp.int32, (BINS, 128), 1)
     for i in range(X):
-        both_pairs = [jnp.where(lax.rem(lane, 64) < 32, acc[2 * i, k:k + 32], acc[2 * i + 1, k:k + 32])
-                      for k in (0, 32)]
-        away = 1 - i % 2
-        both_pairs[away] = pltpu.roll(both_pairs[away], 64, 1)
-        send[i] = jnp.where(lane < 64, both_pairs[0], both_pairs[1])
+        send[i] = jnp.where(lax.rem(lane, 64) < 32, acc[i, 0:32], acc[i, 32:64])
 
     pl.semaphore_wait(barrier, Z - 1 + X * FEAT - 1)
 
@@ -201,19 +198,19 @@
         out_shape=(pltpu.VMEM((16, BINS), jnp.float32), pltpu.VMEM((1, FEAT * PAIRS), jnp.float32)),
         in_specs=[anywhere] * 5,
         out_specs=(vmem, vmem),
-        scratch_shapes=[[pltpu.VMEM((bin_codes.shape[0], rows // CHUNKS), jnp.int32)] * CHUNKS,
+        scratch_shapes=[[pltpu.VMEM((bin_codes.shape[0], c), jnp.int32) for c in CHUNKS],
             pltpu.SMEM((2, FEAT * PAIRS), jnp.int32),
             pltpu.VMEM((1, FEAT * PAIRS), jnp.int32),
             pltpu.VMEM((rows // 128, 128), jnp.bfloat16),
             pltpu.VMEM((rows // 128, 128), jnp.bfloat16),
-            pltpu.VMEM((PAIRS, 64, 128), jnp.float32),
+            pltpu.VMEM((X, 64, 128), jnp.float32),
             pltpu.VMEM((X, BINS, 128), jnp.float32),
             pltpu.VMEM((X, BINS, 128), jnp.float32),
             pltpu.VMEM((Z, BINS, 128), jnp.float32),
             pltpu.VMEM((Z, X, 128), jnp.float32),
             pltpu.VMEM((X, 1, 128), jnp.float32),
             pltpu.VMEM((X * FEAT, 1, 128), jnp.float32),
-            pltpu.SemaphoreType.DMA((CHUNKS,)),
+            pltpu.SemaphoreType.DMA((len(CHUNKS),)),
             pltpu.SemaphoreType.DMA((4,)),
         ] + [pltpu.SemaphoreType.DMA] * 6,
         compiler_params=pltpu.CompilerParams(collective_id=0, has_side_effects=True),

time: 30 us -> 27.6 us (0.920)
  Pallas kernels: 28.1 us -> 25.8 us
    pallas_call x1, Pallas kernels: 28.1 us -> 25.8 us  [shards(): pl.pallas_call(kernel, out_shape=(pltpu.VMEM((16, BINS), jnp.float32), pl...]
where the time goes in v1:
time: 27.6 us; the launch traced here: 27.5 us
  Pallas kernels  25.8 us (93%)
  local copies, waits for them, and re-layouts  1.11 us (4%)
  between operations  0.64 us (2%)
    pallas_call x1, Pallas kernels, shards(): pl.pallas_call(kernel, out_shape=(pltpu.VMEM((16, BINS), jnp.float32), pl...  25.8 us
    unnamed x2, local copies, waits for them, and re-layouts  1.11 us

profile of v1, /device:TPU:1, one launch (start us, length us, event | category | flops | bytes accessed | tf_op | source)
XLA Modules:
  0.0 27.5 jit_solution(14392436615712769020)
XLA Ops:
  0.6 25.8 %shard_map.68 = (f32[16,32]{1,0:T(8,128)S(1)}, f32[1,64]{1,0:T(1,128)S(1)}) custom-call(s32[2,64]{1,0:T(2,128)} %bitcast.8, s32[1,64]{1,0:T(1,128)} %bitcast.9, bf16[64,128]{1,0:T(8,128)(2,1)} %bitcast.6, bf16[64,128]{1,0:T(8,128)(2,1)} %bitcast.7, s32[256,8192]{1,0:T(8,128)} %codes_hbm.1), custom_call_target="tpu_custom_call" | custom-call | tf_op jit(solution)/shard_map/pallas_call | solution.py:196
  26.4 0.6 %copy.9 = f32[16,32]{1,0:T(8,128)} copy(f32[16,32]{1,0:T(8,128)S(1)} %get-tuple-element.6) | data formatting | bytes 4096
  27.0 0.5 %copy.10 = f32[64]{0:T(128)} copy(f32[64]{0:T(128)S(1)} %bitcast.5) | data formatting | bytes 512
